TPU v7x, 32 devices: a whole 2x2x4 slice. The times are simulated.
32 devices in a mesh: group: 2 (over x), head: 2 (over core), blk: 8 (over z, y).
Axes of the slice: x: 2, y: 2, z: 4, core: 2. Of those that a mesh axis runs over, the one named last changes fastest.
Arguments:
- patches: bfloat16 [4096, 1024], P(('group', 'head', 'blk')), parts along dimension 0, may hold values from -60 to 60
- ln_gain: float32 [1024], replicated, may hold values from 0.1 to 1.9
- w_qkv: bfloat16 [1024, 3072], replicated, may hold values from -0.21875 to 0.21875
- qk_gains: float32 [2, 1024], replicated, may hold values from 0.5 to 6
- w_out: bfloat16 [1024, 1024], replicated, may hold values from -0.1875 to 0.1875
Outputs:
- attn_out: bfloat16 [4096, 1024], P(('group', 'head', 'blk')), parts along dimension 0
There are 2 independent parts, one for each index of `group`. A program takes and returns all parts, laid end to end along the dimension named above; an argument that names none is the same for every part. Nothing has to cross between parts.
All inputs are finite; a program needn't handle non-finite values.
Results may differ from a plain program's by a relative error of at most 0.025.
Values may be sent and summed in bfloat16 or wider, within the bound.
A program may use at most 128 MiB of HBM per device.

v0:
```python
import jax
import jax.numpy as jnp
from jax import lax
from jax.sharding import PartitionSpec as P

H = 16
HD = 64


def from_behind(array, axis, by):
    peers = lax.axis_size(axis)
    return lax.ppermute(array, axis, [(i, (i + by) % peers) for i in range(peers)])


def layer_norm(patches, ln_gain):
    values_f = patches.astype(jnp.float32)
    centre = values_f - jnp.mean(values_f, axis=-1, keepdims=True)
    variance = jnp.mean(centre * centre, axis=-1, keepdims=True)
    return (centre * lax.rsqrt(variance + 1e-05) * ln_gain).astype(jnp.bfloat16)


def head_norm(columns, gain_vector, head_count):
    row_count = columns.shape[0]
    shaped = columns.reshape(row_count, head_count, HD)
    square_mean = jnp.mean(shaped * shaped, axis=-1, keepdims=True)
    scaled = shaped * lax.rsqrt(square_mean + 1e-06) * gain_vector.reshape(head_count, HD)
    return scaled.astype(jnp.bfloat16).reshape(row_count, head_count * HD)


def project(normed, weight, gain_query, gain_key, head_count):
    projected = jnp.dot(normed, weight, preferred_element_type=jnp.float32)
    span = head_count * HD
    query = head_norm(projected[:, :span], gain_query, head_count)
    key_rows = head_norm(projected[:, span : 2 * span], gain_key, head_count)
    value_rows = projected[:, 2 * span :].astype(jnp.bfloat16)
    return (query, key_rows, value_rows)


def absorb(query, carried, key_rows, value_rows):
    row_count = key_rows.shape[0]
    head_count = query.shape[1]
    key_blocks = key_rows.reshape(row_count // row_count, row_count, head_count, HD)
    value_blocks = value_rows.reshape(row_count // row_count, row_count, head_count, HD)
    score_scale = HD ** (-0.5)

    def absorb_block(state_now, block_pair):
        running_max, running_sum, weighted = state_now
        key_block, value_block = block_pair
        scores = (
            jnp.einsum("qhd,khd->hqk", query, key_block, preferred_element_type=jnp.float32)
            * score_scale
        )
        new_max = jnp.maximum(running_max, jnp.max(scores, axis=-1))
        shrink = jnp.exp(running_max - new_max)
        exponent = jnp.exp(scores - new_max[:, :, None])
        running_sum = running_sum * shrink + jnp.sum(exponent, axis=-1)
        added = jnp.einsum(
            "hqk,khd->qhd",
            exponent.astype(jnp.bfloat16),
            value_block,
            preferred_element_type=jnp.float32,
        )
        weighted = weighted * shrink.T[:, :, None] + added
        return ((new_max, running_sum, weighted), None)

    return lax.scan(absorb_block, carried, (key_blocks, value_blocks))[0]


def per_device(patches, ln_gain, w_qkv, qk_gains, w_out):
    tok_rows = patches.shape[0]
    head_devices = lax.axis_size("head")
    local_heads = H // head_devices
    local_width = local_heads * HD
    normed = layer_norm(patches, ln_gain)
    query, key_rows, value_rows = project(normed, w_qkv, qk_gains[0], qk_gains[1], H)
    stacked = jnp.stack((query, key_rows, value_rows), axis=1).reshape(
        tok_rows, 3, head_devices, local_width
    )
    regrouped = lax.all_to_all(stacked, "head", split_axis=2, concat_axis=0, tiled=True)
    regrouped = regrouped.reshape(head_devices * tok_rows, 3, local_width)
    query = regrouped[:, 0]
    key_rows = regrouped[:, 1]
    value_rows = regrouped[:, 2]
    query_rows = query.shape[0]
    query = query.reshape(query_rows, local_heads, HD)
    initial = (
        jnp.full((local_heads, query_rows), -jnp.inf, jnp.float32),
        jnp.zeros((local_heads, query_rows), jnp.float32),
        jnp.zeros((query_rows, local_heads, HD), jnp.float32),
    )

    def visit(turn, state_now):
        visitor, running_max, running_sum, weighted = state_now
        running_max, running_sum, weighted = absorb(
            visitor, (running_max, running_sum, weighted), key_rows, value_rows
        )
        visitor = from_behind(visitor, "blk", 1)
        running_max, running_sum, weighted = (
            from_behind(running_max.astype(jnp.bfloat16), "blk", 1).astype(running_max.dtype),
            from_behind(running_sum.astype(jnp.bfloat16), "blk", 1).astype(running_sum.dtype),
            from_behind(weighted.astype(jnp.bfloat16), "blk", 1).astype(weighted.dtype),
        )
        return (visitor, running_max, running_sum, weighted)

    final_state = lax.fori_loop(
        0, lax.axis_size("blk"), visit, (query, initial[0], initial[1], initial[2])
    )
    running_max, running_sum, weighted = (final_state[1], final_state[2], final_state[3])
    attended = (
        (weighted / running_sum.T[:, :, None]).astype(jnp.bfloat16).reshape(query_rows, local_width)
    )
    attended = lax.all_to_all(attended, "head", split_axis=0, concat_axis=1, tiled=True)
    return jnp.dot(attended, w_out, preferred_element_type=jnp.float32).astype(jnp.bfloat16)


def solution(mesh):
    placed = (P(("group", "head", "blk"), None), P(), P(), P(), P())
    return jax.shard_map(
        per_device,
        mesh=mesh,
        in_specs=placed,
        out_specs=P(("group", "head", "blk"), None),
        check_vma=False,
    )
```

profile of v0, /device:TPU:0, one launch (start us, length us, event | category | flops | bytes accessed | tf_op | source)
XLA Modules:
  0.0 165.0 jit_solution(5658059260935367762)
XLA Ops:
  2.4 4.0 %fusion.16 = f32[128,3072]{1,0:T(8,128)S(1)} fusion(bf16[1024,3072]{1,0:T(8,128)(2,1)} %param.9, bf16[128,1024]{1,0:T(8,128)(2,1)} %param.7, f32[1024]{0:T(1024)} %param.8, f32[128]{0:T(128)S(1)} %add_rsqrt_fusion.2, f32[128]{0:T(128)S(1)} %broadcast_multiply_fusion), kind=kOutput, calls=%fused_computation.32 | convolution fusion | flops 805961728 | bytes 8131584 | tf_op jit(solution)/shard_map/dot_general | solution.py:31
  10.7 2.1 %copy.37 = f32[128,1024]{0,1:T(8,128)} copy(f32[128,1024]{1,0:T(8,128)} %get-tuple-element.133) | data formatting | bytes 1048576 | tf_op jit(solution)/shard_map/mul | solution.py:25
  15.4 3.5 %all-to-all-start = ((bf16[128,3,2,512]{0,3,1,2:T(8,128)(2,1)}), bf16[128,3,2,512]{0,3,1,2:T(8,128)(2,1)S(1)}, u32[]{:S(2)}, u32[]{:S(2)}) async-start(bf16[128,3,2,512]{0,3,1,2:T(8,128)(2,1)} %copy.42), calls=%async_computation | async-start | bytes 1572864 | tf_op jit(solution)/shard_map/all_to_all | solution.py:79
  18.9 1.9 %all-to-all-done = bf16[128,3,2,512]{0,3,1,2:T(8,128)(2,1)S(1)} async-done(((bf16[128,3,2,512]{0,3,1,2:T(8,128)(2,1)}), bf16[128,3,2,512]{0,3,1,2:T(8,128)(2,1)S(1)}, u32[]{:S(2)}, u32[]{:S(2)}) %all-to-all-start) | async-done | bytes 786464 | tf_op jit(solution)/shard_map/all_to_all | solution.py:79
  22.0 1.9 %fusion.21 = (bf16[256,1,512]{2,0,1:T(8,128)(2,1)S(1)}, bf16[256,1,512]{2,0,1:T(8,128)(2,1)}, bf16[256,1,512]{2,0,1:T(8,128)(2,1)S(1)}) fusion(bf16[256,3,512]{2,0,1:T(8,128)(2,1)} %bitcast.54), kind=kLoop, calls=%fused_computation.44 | loop fusion | bytes 1572864 | tf_op jit(solution)/shard_map/slice | solution.py:83
  25.9 133.8 %while.16 = (s32[]{:T(128)}, bf16[256,8,64]{0,2,1:T(8,128)(2,1)S(1)}, f32[8,256]{1,0:T(8,128)S(1)}, f32[8,256]{1,0:T(8,128)S(1)}, f32[256,8,64]{0,2,1:T(8,128)S(...) while((s32[]{:T(128)}, ...), condition=%wide.region_7.8_spmd.clone, body=%wide.region_4.7_spmd.clone.sunk | while | flops 139087872 | bytes 19833124 | solution.py:105
  26.0 3.0 %collective-permute-start = (bf16[256,8,64]{0,2,1:T(8,128)(2,1)S(1)}, bf16[256,8,64]{0,2,1:T(8,128)(2,1)S(1)}, u32[]{:S(2)}, u32[]{:S(2)}) collective-permute-start(bf16[256,8,64]{0,2,1:T(8,128)(2,1)S(1)} %copy.58), channel_id=1, source_target_pairs={{0,1},{1,2},{2,3},{3,4},{4,5},{5,6},{6,7},{7,0},{8,9},{9,10},{10,1... | collective-permute-start | bytes 786440 | tf_op jit(solution)/shard_map/while/body/eval_jaxpr/ppermute | solution.py:12
  30.8 3.0 %fusion.43 = bf16[256,8,64]{0,2,1:T(8,128)(2,1)} fusion(bf16[256,8,64]{0,2,1:T(8,128)(2,1)} %bitcast.53, f32[8,256,256]{1,2,0:T(8,128)} %get-tuple-element.191, f32[8,256]{1,0:T(8,128)S(1)} %get-tuple-element.193, f32[256,8,64]{0,2,1:T(8,128)S(1)} %get-tuple-element.210, f32[256,8]{0,1:T(8,128)S(1)} %get-tuple-element.196, pred[]{:T(512)S(6)} %compare.3), kind=kOutput, calls=%fused_computation.6.clone.1 | convolution fusion | flops 69206016 | bytes 3162113 | tf_op jit(solution)/shard_map/while/body/eval_jaxpr/while/body/eval_jaxpr/hqk,khd->qhd/dot_general | solution.py:57
  38.9 6.2 %collective-permute-done.1 = bf16[8,256]{1,0:T(8,128)(2,1)S(1)} collective-permute-done((bf16[8,256]{1,0:T(8,128)(2,1)S(1)}, bf16[8,256]{1,0:T(8,128)(2,1)S(1)}, u32[]{:S(2)}, u32[]{:S(2)}) %collective-permute-start.1) | collective-permute-done | bytes 4128 | tf_op jit(solution)/shard_map/while/body/eval_jaxpr/ppermute | solution.py:12
  48.0 3.0 %fusion.43 = bf16[256,8,64]{0,2,1:T(8,128)(2,1)} fusion(bf16[256,8,64]{0,2,1:T(8,128)(2,1)} %bitcast.53, f32[8,256,256]{1,2,0:T(8,128)} %get-tuple-element.191, f32[8,256]{1,0:T(8,128)S(1)} %get-tuple-element.193, f32[256,8,64]{0,2,1:T(8,128)S(1)} %get-tuple-element.210, f32[256,8]{0,1:T(8,128)S(1)} %get-tuple-element.196, pred[]{:T(512)S(6)} %compare.3), kind=kOutput, calls=%fused_computation.6.clone.1 | convolution fusion | flops 69206016 | bytes 3162113 | tf_op jit(solution)/shard_map/while/body/eval_jaxpr/while/body/eval_jaxpr/hqk,khd->qhd/dot_general | solution.py:57
  53.3 2.4 %collective-permute-start.2 = (bf16[8,256]{1,0:T(8,128)(2,1)S(1)}, bf16[8,256]{1,0:T(8,128)(2,1)S(1)}, u32[]{:S(2)}, u32[]{:S(2)}) collective-permute-start(bf16[8,256]{1,0:T(8,128)(2,1)S(1)} %get-tuple-element.195), channel_id=1, source_target_pairs={{0,1},{1,2},{2,3},{3,4},{4,5},{5,6},{6,7},{7,0},{8,9},{9,10},{10,1... | collective-permute-start | bytes 12296 | tf_op jit(solution)/shard_map/while/body/eval_jaxpr/ppermute | solution.py:12
  55.8 6.2 %collective-permute-done.1 = bf16[8,256]{1,0:T(8,128)(2,1)S(1)} collective-permute-done((bf16[8,256]{1,0:T(8,128)(2,1)S(1)}, bf16[8,256]{1,0:T(8,128)(2,1)S(1)}, u32[]{:S(2)}, u32[]{:S(2)}) %collective-permute-start.1) | collective-permute-done | bytes 4128 | tf_op jit(solution)/shard_map/while/body/eval_jaxpr/ppermute | solution.py:12
  63.1 1.8 %multiply_reduce_fusion.2 = (f32[8,256]{1,0:T(8,128)S(1)}, f32[8,256,256]{1,2,0:T(8,128)}) fusion(bf16[256,8,64]{0,2,1:T(8,128)(2,1)S(1)} %copy.58, bf16[256,8,64]{0,2,1:T(8,128)(2,1)S(1)} %bitcast.51), kind=kOutput, calls=%fused_computation.1.clone.1 | convolution fusion | flops 68155392 | bytes 2629632 | tf_op jit(solution)/shard_map/while/body/eval_jaxpr/while/body/eval_jaxpr/qhd,khd->hqk/dot_general | solution.py:50
  64.9 3.0 %fusion.43 = bf16[256,8,64]{0,2,1:T(8,128)(2,1)} fusion(bf16[256,8,64]{0,2,1:T(8,128)(2,1)} %bitcast.53, f32[8,256,256]{1,2,0:T(8,128)} %get-tuple-element.191, f32[8,256]{1,0:T(8,128)S(1)} %get-tuple-element.193, f32[256,8,64]{0,2,1:T(8,128)S(1)} %get-tuple-element.210, f32[256,8]{0,1:T(8,128)S(1)} %get-tuple-element.196, pred[]{:T(512)S(6)} %compare.3), kind=kOutput, calls=%fused_computation.6.clone.1 | convolution fusion | flops 69206016 | bytes 3162113 | tf_op jit(solution)/shard_map/while/body/eval_jaxpr/while/body/eval_jaxpr/hqk,khd->qhd/dot_general | solution.py:57
  70.9 7.6 %collective-permute-done.1 = bf16[8,256]{1,0:T(8,128)(2,1)S(1)} collective-permute-done((bf16[8,256]{1,0:T(8,128)(2,1)S(1)}, bf16[8,256]{1,0:T(8,128)(2,1)S(1)}, u32[]{:S(2)}, u32[]{:S(2)}) %collective-permute-start.1) | collective-permute-done | bytes 4128 | tf_op jit(solution)/shard_map/while/body/eval_jaxpr/ppermute | solution.py:12
  79.6 1.8 %multiply_reduce_fusion.2 = (f32[8,256]{1,0:T(8,128)S(1)}, f32[8,256,256]{1,2,0:T(8,128)}) fusion(bf16[256,8,64]{0,2,1:T(8,128)(2,1)S(1)} %copy.58, bf16[256,8,64]{0,2,1:T(8,128)(2,1)S(1)} %bitcast.51), kind=kOutput, calls=%fused_computation.1.clone.1 | convolution fusion | flops 68155392 | bytes 2629632 | tf_op jit(solution)/shard_map/while/body/eval_jaxpr/while/body/eval_jaxpr/qhd,khd->hqk/dot_general | solution.py:50
  81.5 3.0 %fusion.43 = bf16[256,8,64]{0,2,1:T(8,128)(2,1)} fusion(bf16[256,8,64]{0,2,1:T(8,128)(2,1)} %bitcast.53, f32[8,256,256]{1,2,0:T(8,128)} %get-tuple-element.191, f32[8,256]{1,0:T(8,128)S(1)} %get-tuple-element.193, f32[256,8,64]{0,2,1:T(8,128)S(1)} %get-tuple-element.210, f32[256,8]{0,1:T(8,128)S(1)} %get-tuple-element.196, pred[]{:T(512)S(6)} %compare.3), kind=kOutput, calls=%fused_computation.6.clone.1 | convolution fusion | flops 69206016 | bytes 3162113 | tf_op jit(solution)/shard_map/while/body/eval_jaxpr/while/body/eval_jaxpr/hqk,khd->qhd/dot_general | solution.py:57
  85.0 2.0 %collective-permute-start.2 = (bf16[8,256]{1,0:T(8,128)(2,1)S(1)}, bf16[8,256]{1,0:T(8,128)(2,1)S(1)}, u32[]{:S(2)}, u32[]{:S(2)}) collective-permute-start(bf16[8,256]{1,0:T(8,128)(2,1)S(1)} %get-tuple-element.195), channel_id=1, source_target_pairs={{0,1},{1,2},{2,3},{3,4},{4,5},{5,6},{6,7},{7,0},{8,9},{9,10},{10,1... | collective-permute-start | bytes 12296 | tf_op jit(solution)/shard_map/while/body/eval_jaxpr/ppermute | solution.py:12
  86.9 7.8 %collective-permute-done.1 = bf16[8,256]{1,0:T(8,128)(2,1)S(1)} collective-permute-done((bf16[8,256]{1,0:T(8,128)(2,1)S(1)}, bf16[8,256]{1,0:T(8,128)(2,1)S(1)}, u32[]{:S(2)}, u32[]{:S(2)}) %collective-permute-start.1) | collective-permute-done | bytes 4128 | tf_op jit(solution)/shard_map/while/body/eval_jaxpr/ppermute | solution.py:12
  97.7 3.0 %fusion.43 = bf16[256,8,64]{0,2,1:T(8,128)(2,1)} fusion(bf16[256,8,64]{0,2,1:T(8,128)(2,1)} %bitcast.53, f32[8,256,256]{1,2,0:T(8,128)} %get-tuple-element.191, f32[8,256]{1,0:T(8,128)S(1)} %get-tuple-element.193, f32[256,8,64]{0,2,1:T(8,128)S(1)} %get-tuple-element.210, f32[256,8]{0,1:T(8,128)S(1)} %get-tuple-element.196, pred[]{:T(512)S(6)} %compare.3), kind=kOutput, calls=%fused_computation.6.clone.1 | convolution fusion | flops 69206016 | bytes 3162113 | tf_op jit(solution)/shard_map/while/body/eval_jaxpr/while/body/eval_jaxpr/hqk,khd->qhd/dot_general | solution.py:57
  101.2 2.3 %collective-permute-start.2 = (bf16[8,256]{1,0:T(8,128)(2,1)S(1)}, bf16[8,256]{1,0:T(8,128)(2,1)S(1)}, u32[]{:S(2)}, u32[]{:S(2)}) collective-permute-start(bf16[8,256]{1,0:T(8,128)(2,1)S(1)} %get-tuple-element.195), channel_id=1, source_target_pairs={{0,1},{1,2},{2,3},{3,4},{4,5},{5,6},{6,7},{7,0},{8,9},{9,10},{10,1... | collective-permute-start | bytes 12296 | tf_op jit(solution)/shard_map/while/body/eval_jaxpr/ppermute | solution.py:12
  103.5 7.2 %collective-permute-done.1 = bf16[8,256]{1,0:T(8,128)(2,1)S(1)} collective-permute-done((bf16[8,256]{1,0:T(8,128)(2,1)S(1)}, bf16[8,256]{1,0:T(8,128)(2,1)S(1)}, u32[]{:S(2)}, u32[]{:S(2)}) %collective-permute-start.1) | collective-permute-done | bytes 4128 | tf_op jit(solution)/shard_map/while/body/eval_jaxpr/ppermute | solution.py:12
  113.7 3.0 %fusion.43 = bf16[256,8,64]{0,2,1:T(8,128)(2,1)} fusion(bf16[256,8,64]{0,2,1:T(8,128)(2,1)} %bitcast.53, f32[8,256,256]{1,2,0:T(8,128)} %get-tuple-element.191, f32[8,256]{1,0:T(8,128)S(1)} %get-tuple-element.193, f32[256,8,64]{0,2,1:T(8,128)S(1)} %get-tuple-element.210, f32[256,8]{0,1:T(8,128)S(1)} %get-tuple-element.196, pred[]{:T(512)S(6)} %compare.3), kind=kOutput, calls=%fused_computation.6.clone.1 | convolution fusion | flops 69206016 | bytes 3162113 | tf_op jit(solution)/shard_map/while/body/eval_jaxpr/while/body/eval_jaxpr/hqk,khd->qhd/dot_general | solution.py:57
  117.2 2.5 %collective-permute-start.2 = (bf16[8,256]{1,0:T(8,128)(2,1)S(1)}, bf16[8,256]{1,0:T(8,128)(2,1)S(1)}, u32[]{:S(2)}, u32[]{:S(2)}) collective-permute-start(bf16[8,256]{1,0:T(8,128)(2,1)S(1)} %get-tuple-element.195), channel_id=1, source_target_pairs={{0,1},{1,2},{2,3},{3,4},{4,5},{5,6},{6,7},{7,0},{8,9},{9,10},{10,1... | collective-permute-start | bytes 12296 | tf_op jit(solution)/shard_map/while/body/eval_jaxpr/ppermute | solution.py:12
  119.7 7.0 %collective-permute-done.1 = bf16[8,256]{1,0:T(8,128)(2,1)S(1)} collective-permute-done((bf16[8,256]{1,0:T(8,128)(2,1)S(1)}, bf16[8,256]{1,0:T(8,128)(2,1)S(1)}, u32[]{:S(2)}, u32[]{:S(2)}) %collective-permute-start.1) | collective-permute-done | bytes 4128 | tf_op jit(solution)/shard_map/while/body/eval_jaxpr/ppermute | solution.py:12
  129.7 3.0 %fusion.43 = bf16[256,8,64]{0,2,1:T(8,128)(2,1)} fusion(bf16[256,8,64]{0,2,1:T(8,128)(2,1)} %bitcast.53, f32[8,256,256]{1,2,0:T(8,128)} %get-tuple-element.191, f32[8,256]{1,0:T(8,128)S(1)} %get-tuple-element.193, f32[256,8,64]{0,2,1:T(8,128)S(1)} %get-tuple-element.210, f32[256,8]{0,1:T(8,128)S(1)} %get-tuple-element.196, pred[]{:T(512)S(6)} %compare.3), kind=kOutput, calls=%fused_computation.6.clone.1 | convolution fusion | flops 69206016 | bytes 3162113 | tf_op jit(solution)/shard_map/while/body/eval_jaxpr/while/body/eval_jaxpr/hqk,khd->qhd/dot_general | solution.py:57
  133.2 2.5 %collective-permute-start.2 = (bf16[8,256]{1,0:T(8,128)(2,1)S(1)}, bf16[8,256]{1,0:T(8,128)(2,1)S(1)}, u32[]{:S(2)}, u32[]{:S(2)}) collective-permute-start(bf16[8,256]{1,0:T(8,128)(2,1)S(1)} %get-tuple-element.195), channel_id=1, source_target_pairs={{0,1},{1,2},{2,3},{3,4},{4,5},{5,6},{6,7},{7,0},{8,9},{9,10},{10,1... | collective-permute-start | bytes 12296 | tf_op jit(solution)/shard_map/while/body/eval_jaxpr/ppermute | solution.py:12
  135.7 7.0 %collective-permute-done.1 = bf16[8,256]{1,0:T(8,128)(2,1)S(1)} collective-permute-done((bf16[8,256]{1,0:T(8,128)(2,1)S(1)}, bf16[8,256]{1,0:T(8,128)(2,1)S(1)}, u32[]{:S(2)}, u32[]{:S(2)}) %collective-permute-start.1) | collective-permute-done | bytes 4128 | tf_op jit(solution)/shard_map/while/body/eval_jaxpr/ppermute | solution.py:12
  145.7 3.0 %fusion.43 = bf16[256,8,64]{0,2,1:T(8,128)(2,1)} fusion(bf16[256,8,64]{0,2,1:T(8,128)(2,1)} %bitcast.53, f32[8,256,256]{1,2,0:T(8,128)} %get-tuple-element.191, f32[8,256]{1,0:T(8,128)S(1)} %get-tuple-element.193, f32[256,8,64]{0,2,1:T(8,128)S(1)} %get-tuple-element.210, f32[256,8]{0,1:T(8,128)S(1)} %get-tuple-element.196, pred[]{:T(512)S(6)} %compare.3), kind=kOutput, calls=%fused_computation.6.clone.1 | convolution fusion | flops 69206016 | bytes 3162113 | tf_op jit(solution)/shard_map/while/body/eval_jaxpr/while/body/eval_jaxpr/hqk,khd->qhd/dot_general | solution.py:57
  149.2 2.5 %collective-permute-start.2 = (bf16[8,256]{1,0:T(8,128)(2,1)S(1)}, bf16[8,256]{1,0:T(8,128)(2,1)S(1)}, u32[]{:S(2)}, u32[]{:S(2)}) collective-permute-start(bf16[8,256]{1,0:T(8,128)(2,1)S(1)} %get-tuple-element.195), channel_id=1, source_target_pairs={{0,1},{1,2},{2,3},{3,4},{4,5},{5,6},{6,7},{7,0},{8,9},{9,10},{10,1... | collective-permute-start | bytes 12296 | tf_op jit(solution)/shard_map/while/body/eval_jaxpr/ppermute | solution.py:12
  151.7 7.0 %collective-permute-done.1 = bf16[8,256]{1,0:T(8,128)(2,1)S(1)} collective-permute-done((bf16[8,256]{1,0:T(8,128)(2,1)S(1)}, bf16[8,256]{1,0:T(8,128)(2,1)S(1)}, u32[]{:S(2)}, u32[]{:S(2)}) %collective-permute-start.1) | collective-permute-done | bytes 4128 | tf_op jit(solution)/shard_map/while/body/eval_jaxpr/ppermute | solution.py:12
  159.9 3.9 %all_to_all.34 = bf16[2,128,512]{1,2,0:T(8,128)(2,1)S(1)} all-to-all(bf16[2,128,512]{1,2,0:T(8,128)(2,1)S(1)} %copy.47), channel_id=1, replica_groups=mesh['group'=2,'head'=2,'blk'=8] {'head'}, dimensions={0} | all-to-all | bytes 524288 | tf_op jit(solution)/shard_map/all_to_all | solution.py:112
  (164 shorter events, 45.7 us)
Async XLA Ops:
  26.0 20.1 %collective-permute-start = (bf16[256,8,64]{0,2,1:T(8,128)(2,1)S(1)}, bf16[256,8,64]{0,2,1:T(8,128)(2,1)S(1)}, u32[]{:S(2)}, u32[]{:S(2)}) collective-permute-start(bf16[256,8,64]{0,2,1:T(8,128)(2,1)S(1)} %copy.58), channel_id=1, source_target_pairs={{0,1},{1,2},{2,3},{3,4},{4,5},{5,6},{6,7},{7,0},{8,9},{9,10},{10,1... | collective-permute-start | bytes 786440 | tf_op jit(solution)/shard_map/while/body/eval_jaxpr/ppermute | solution.py:12
  33.9 11.2 %collective-permute-start.3 = (bf16[256,8,64]{0,2,1:T(8,128)(2,1)}, bf16[256,8,64]{0,2,1:T(8,128)(2,1)}, u32[]{:S(2)}, u32[]{:S(2)}) collective-permute-start(bf16[256,8,64]{0,2,1:T(8,128)(2,1)} %fusion.43), channel_id=1, source_target_pairs={{0,1},{1,2},{2,3},{3,4},{4,5},{5,6},{6,7},{7,0},{8,9},{9,10},{10,1... | collective-permute-start | bytes 786440 | tf_op jit(solution)/shard_map/while/body/eval_jaxpr/ppermute | solution.py:12
  35.8 9.3 %collective-permute-start.1 = (bf16[8,256]{1,0:T(8,128)(2,1)S(1)}, bf16[8,256]{1,0:T(8,128)(2,1)S(1)}, u32[]{:S(2)}, u32[]{:S(2)}) collective-permute-start(bf16[8,256]{1,0:T(8,128)(2,1)S(1)} %get-tuple-element.194), channel_id=1, source_target_pairs={{0,1},{1,2},{2,3},{3,4},{4,5},{5,6},{6,7},{7,0},{8,9},{9,10},{10,1... | collective-permute-start | bytes 12296 | tf_op jit(solution)/shard_map/while/body/eval_jaxpr/ppermute | solution.py:12
  37.3 7.7 %collective-permute-start.2 = (bf16[8,256]{1,0:T(8,128)(2,1)S(1)}, bf16[8,256]{1,0:T(8,128)(2,1)S(1)}, u32[]{:S(2)}, u32[]{:S(2)}) collective-permute-start(bf16[8,256]{1,0:T(8,128)(2,1)S(1)} %get-tuple-element.195), channel_id=1, source_target_pairs={{0,1},{1,2},{2,3},{3,4},{4,5},{5,6},{6,7},{7,0},{8,9},{9,10},{10,1... | collective-permute-start | bytes 12296 | tf_op jit(solution)/shard_map/while/body/eval_jaxpr/ppermute | solution.py:12
  46.1 16.9 %collective-permute-start = (bf16[256,8,64]{0,2,1:T(8,128)(2,1)S(1)}, bf16[256,8,64]{0,2,1:T(8,128)(2,1)S(1)}, u32[]{:S(2)}, u32[]{:S(2)}) collective-permute-start(bf16[256,8,64]{0,2,1:T(8,128)(2,1)S(1)} %copy.58), channel_id=1, source_target_pairs={{0,1},{1,2},{2,3},{3,4},{4,5},{5,6},{6,7},{7,0},{8,9},{9,10},{10,1... | collective-permute-start | bytes 786440 | tf_op jit(solution)/shard_map/while/body/eval_jaxpr/ppermute | solution.py:12
  51.1 10.9 %collective-permute-start.3 = (bf16[256,8,64]{0,2,1:T(8,128)(2,1)}, bf16[256,8,64]{0,2,1:T(8,128)(2,1)}, u32[]{:S(2)}, u32[]{:S(2)}) collective-permute-start(bf16[256,8,64]{0,2,1:T(8,128)(2,1)} %fusion.43), channel_id=1, source_target_pairs={{0,1},{1,2},{2,3},{3,4},{4,5},{5,6},{6,7},{7,0},{8,9},{9,10},{10,1... | collective-permute-start | bytes 786440 | tf_op jit(solution)/shard_map/while/body/eval_jaxpr/ppermute | solution.py:12
  52.7 9.3 %collective-permute-start.1 = (bf16[8,256]{1,0:T(8,128)(2,1)S(1)}, bf16[8,256]{1,0:T(8,128)(2,1)S(1)}, u32[]{:S(2)}, u32[]{:S(2)}) collective-permute-start(bf16[8,256]{1,0:T(8,128)(2,1)S(1)} %get-tuple-element.194), channel_id=1, source_target_pairs={{0,1},{1,2},{2,3},{3,4},{4,5},{5,6},{6,7},{7,0},{8,9},{9,10},{10,1... | collective-permute-start | bytes 12296 | tf_op jit(solution)/shard_map/while/body/eval_jaxpr/ppermute | solution.py:12
  53.3 8.6 %collective-permute-start.2 = (bf16[8,256]{1,0:T(8,128)(2,1)S(1)}, bf16[8,256]{1,0:T(8,128)(2,1)S(1)}, u32[]{:S(2)}, u32[]{:S(2)}) collective-permute-start(bf16[8,256]{1,0:T(8,128)(2,1)S(1)} %get-tuple-element.195), channel_id=1, source_target_pairs={{0,1},{1,2},{2,3},{3,4},{4,5},{5,6},{6,7},{7,0},{8,9},{9,10},{10,1... | collective-permute-start | bytes 12296 | tf_op jit(solution)/shard_map/while/body/eval_jaxpr/ppermute | solution.py:12
  63.0 16.5 %collective-permute-start = (bf16[256,8,64]{0,2,1:T(8,128)(2,1)S(1)}, bf16[256,8,64]{0,2,1:T(8,128)(2,1)S(1)}, u32[]{:S(2)}, u32[]{:S(2)}) collective-permute-start(bf16[256,8,64]{0,2,1:T(8,128)(2,1)S(1)} %copy.58), channel_id=1, source_target_pairs={{0,1},{1,2},{2,3},{3,4},{4,5},{5,6},{6,7},{7,0},{8,9},{9,10},{10,1... | collective-permute-start | bytes 786440 | tf_op jit(solution)/shard_map/while/body/eval_jaxpr/ppermute | solution.py:12
  68.0 10.5 %collective-permute-start.3 = (bf16[256,8,64]{0,2,1:T(8,128)(2,1)}, bf16[256,8,64]{0,2,1:T(8,128)(2,1)}, u32[]{:S(2)}, u32[]{:S(2)}) collective-permute-start(bf16[256,8,64]{0,2,1:T(8,128)(2,1)} %fusion.43), channel_id=1, source_target_pairs={{0,1},{1,2},{2,3},{3,4},{4,5},{5,6},{6,7},{7,0},{8,9},{9,10},{10,1... | collective-permute-start | bytes 786440 | tf_op jit(solution)/shard_map/while/body/eval_jaxpr/ppermute | solution.py:12
  68.4 10.1 %collective-permute-start.1 = (bf16[8,256]{1,0:T(8,128)(2,1)S(1)}, bf16[8,256]{1,0:T(8,128)(2,1)S(1)}, u32[]{:S(2)}, u32[]{:S(2)}) collective-permute-start(bf16[8,256]{1,0:T(8,128)(2,1)S(1)} %get-tuple-element.194), channel_id=1, source_target_pairs={{0,1},{1,2},{2,3},{3,4},{4,5},{5,6},{6,7},{7,0},{8,9},{9,10},{10,1... | collective-permute-start | bytes 12296 | tf_op jit(solution)/shard_map/while/body/eval_jaxpr/ppermute | solution.py:12
  69.2 9.3 %collective-permute-start.2 = (bf16[8,256]{1,0:T(8,128)(2,1)S(1)}, bf16[8,256]{1,0:T(8,128)(2,1)S(1)}, u32[]{:S(2)}, u32[]{:S(2)}) collective-permute-start(bf16[8,256]{1,0:T(8,128)(2,1)S(1)} %get-tuple-element.195), channel_id=1, source_target_pairs={{0,1},{1,2},{2,3},{3,4},{4,5},{5,6},{6,7},{7,0},{8,9},{9,10},{10,1... | collective-permute-start | bytes 12296 | tf_op jit(solution)/shard_map/while/body/eval_jaxpr/ppermute | solution.py:12
  79.6 16.2 %collective-permute-start = (bf16[256,8,64]{0,2,1:T(8,128)(2,1)S(1)}, bf16[256,8,64]{0,2,1:T(8,128)(2,1)S(1)}, u32[]{:S(2)}, u32[]{:S(2)}) collective-permute-start(bf16[256,8,64]{0,2,1:T(8,128)(2,1)S(1)} %copy.58), channel_id=1, source_target_pairs={{0,1},{1,2},{2,3},{3,4},{4,5},{5,6},{6,7},{7,0},{8,9},{9,10},{10,1... | collective-permute-start | bytes 786440 | tf_op jit(solution)/shard_map/while/body/eval_jaxpr/ppermute | solution.py:12
  84.5 10.2 %collective-permute-start.3 = (bf16[256,8,64]{0,2,1:T(8,128)(2,1)}, bf16[256,8,64]{0,2,1:T(8,128)(2,1)}, u32[]{:S(2)}, u32[]{:S(2)}) collective-permute-start(bf16[256,8,64]{0,2,1:T(8,128)(2,1)} %fusion.43), channel_id=1, source_target_pairs={{0,1},{1,2},{2,3},{3,4},{4,5},{5,6},{6,7},{7,0},{8,9},{9,10},{10,1... | collective-permute-start | bytes 786440 | tf_op jit(solution)/shard_map/while/body/eval_jaxpr/ppermute | solution.py:12
  84.9 9.8 %collective-permute-start.1 = (bf16[8,256]{1,0:T(8,128)(2,1)S(1)}, bf16[8,256]{1,0:T(8,128)(2,1)S(1)}, u32[]{:S(2)}, u32[]{:S(2)}) collective-permute-start(bf16[8,256]{1,0:T(8,128)(2,1)S(1)} %get-tuple-element.194), channel_id=1, source_target_pairs={{0,1},{1,2},{2,3},{3,4},{4,5},{5,6},{6,7},{7,0},{8,9},{9,10},{10,1... | collective-permute-start | bytes 12296 | tf_op jit(solution)/shard_map/while/body/eval_jaxpr/ppermute | solution.py:12
  85.0 9.7 %collective-permute-start.2 = (bf16[8,256]{1,0:T(8,128)(2,1)S(1)}, bf16[8,256]{1,0:T(8,128)(2,1)S(1)}, u32[]{:S(2)}, u32[]{:S(2)}) collective-permute-start(bf16[8,256]{1,0:T(8,128)(2,1)S(1)} %get-tuple-element.195), channel_id=1, source_target_pairs={{0,1},{1,2},{2,3},{3,4},{4,5},{5,6},{6,7},{7,0},{8,9},{9,10},{10,1... | collective-permute-start | bytes 12296 | tf_op jit(solution)/shard_map/while/body/eval_jaxpr/ppermute | solution.py:12
  95.8 15.9 %collective-permute-start = (bf16[256,8,64]{0,2,1:T(8,128)(2,1)S(1)}, bf16[256,8,64]{0,2,1:T(8,128)(2,1)S(1)}, u32[]{:S(2)}, u32[]{:S(2)}) collective-permute-start(bf16[256,8,64]{0,2,1:T(8,128)(2,1)S(1)} %copy.58), channel_id=1, source_target_pairs={{0,1},{1,2},{2,3},{3,4},{4,5},{5,6},{6,7},{7,0},{8,9},{9,10},{10,1... | collective-permute-start | bytes 786440 | tf_op jit(solution)/shard_map/while/body/eval_jaxpr/ppermute | solution.py:12
  100.7 10.0 %collective-permute-start.3 = (bf16[256,8,64]{0,2,1:T(8,128)(2,1)}, bf16[256,8,64]{0,2,1:T(8,128)(2,1)}, u32[]{:S(2)}, u32[]{:S(2)}) collective-permute-start(bf16[256,8,64]{0,2,1:T(8,128)(2,1)} %fusion.43), channel_id=1, source_target_pairs={{0,1},{1,2},{2,3},{3,4},{4,5},{5,6},{6,7},{7,0},{8,9},{9,10},{10,1... | collective-permute-start | bytes 786440 | tf_op jit(solution)/shard_map/while/body/eval_jaxpr/ppermute | solution.py:12
  101.1 9.6 %collective-permute-start.1 = (bf16[8,256]{1,0:T(8,128)(2,1)S(1)}, bf16[8,256]{1,0:T(8,128)(2,1)S(1)}, u32[]{:S(2)}, u32[]{:S(2)}) collective-permute-start(bf16[8,256]{1,0:T(8,128)(2,1)S(1)} %get-tuple-element.194), channel_id=1, source_target_pairs={{0,1},{1,2},{2,3},{3,4},{4,5},{5,6},{6,7},{7,0},{8,9},{9,10},{10,1... | collective-permute-start | bytes 12296 | tf_op jit(solution)/shard_map/while/body/eval_jaxpr/ppermute | solution.py:12
  101.2 9.5 %collective-permute-start.2 = (bf16[8,256]{1,0:T(8,128)(2,1)S(1)}, bf16[8,256]{1,0:T(8,128)(2,1)S(1)}, u32[]{:S(2)}, u32[]{:S(2)}) collective-permute-start(bf16[8,256]{1,0:T(8,128)(2,1)S(1)} %get-tuple-element.195), channel_id=1, source_target_pairs={{0,1},{1,2},{2,3},{3,4},{4,5},{5,6},{6,7},{7,0},{8,9},{9,10},{10,1... | collective-permute-start | bytes 12296 | tf_op jit(solution)/shard_map/while/body/eval_jaxpr/ppermute | solution.py:12
  111.8 15.9 %collective-permute-start = (bf16[256,8,64]{0,2,1:T(8,128)(2,1)S(1)}, bf16[256,8,64]{0,2,1:T(8,128)(2,1)S(1)}, u32[]{:S(2)}, u32[]{:S(2)}) collective-permute-start(bf16[256,8,64]{0,2,1:T(8,128)(2,1)S(1)} %copy.58), channel_id=1, source_target_pairs={{0,1},{1,2},{2,3},{3,4},{4,5},{5,6},{6,7},{7,0},{8,9},{9,10},{10,1... | collective-permute-start | bytes 786440 | tf_op jit(solution)/shard_map/while/body/eval_jaxpr/ppermute | solution.py:12
  116.7 10.0 %collective-permute-start.3 = (bf16[256,8,64]{0,2,1:T(8,128)(2,1)}, bf16[256,8,64]{0,2,1:T(8,128)(2,1)}, u32[]{:S(2)}, u32[]{:S(2)}) collective-permute-start(bf16[256,8,64]{0,2,1:T(8,128)(2,1)} %fusion.43), channel_id=1, source_target_pairs={{0,1},{1,2},{2,3},{3,4},{4,5},{5,6},{6,7},{7,0},{8,9},{9,10},{10,1... | collective-permute-start | bytes 786440 | tf_op jit(solution)/shard_map/while/body/eval_jaxpr/ppermute | solution.py:12
  117.1 9.6 %collective-permute-start.1 = (bf16[8,256]{1,0:T(8,128)(2,1)S(1)}, bf16[8,256]{1,0:T(8,128)(2,1)S(1)}, u32[]{:S(2)}, u32[]{:S(2)}) collective-permute-start(bf16[8,256]{1,0:T(8,128)(2,1)S(1)} %get-tuple-element.194), channel_id=1, source_target_pairs={{0,1},{1,2},{2,3},{3,4},{4,5},{5,6},{6,7},{7,0},{8,9},{9,10},{10,1... | collective-permute-start | bytes 12296 | tf_op jit(solution)/shard_map/while/body/eval_jaxpr/ppermute | solution.py:12
  117.2 9.5 %collective-permute-start.2 = (bf16[8,256]{1,0:T(8,128)(2,1)S(1)}, bf16[8,256]{1,0:T(8,128)(2,1)S(1)}, u32[]{:S(2)}, u32[]{:S(2)}) collective-permute-start(bf16[8,256]{1,0:T(8,128)(2,1)S(1)} %get-tuple-element.195), channel_id=1, source_target_pairs={{0,1},{1,2},{2,3},{3,4},{4,5},{5,6},{6,7},{7,0},{8,9},{9,10},{10,1... | collective-permute-start | bytes 12296 | tf_op jit(solution)/shard_map/while/body/eval_jaxpr/ppermute | solution.py:12
  127.8 15.9 %collective-permute-start = (bf16[256,8,64]{0,2,1:T(8,128)(2,1)S(1)}, bf16[256,8,64]{0,2,1:T(8,128)(2,1)S(1)}, u32[]{:S(2)}, u32[]{:S(2)}) collective-permute-start(bf16[256,8,64]{0,2,1:T(8,128)(2,1)S(1)} %copy.58), channel_id=1, source_target_pairs={{0,1},{1,2},{2,3},{3,4},{4,5},{5,6},{6,7},{7,0},{8,9},{9,10},{10,1... | collective-permute-start | bytes 786440 | tf_op jit(solution)/shard_map/while/body/eval_jaxpr/ppermute | solution.py:12
  132.7 10.0 %collective-permute-start.3 = (bf16[256,8,64]{0,2,1:T(8,128)(2,1)}, bf16[256,8,64]{0,2,1:T(8,128)(2,1)}, u32[]{:S(2)}, u32[]{:S(2)}) collective-permute-start(bf16[256,8,64]{0,2,1:T(8,128)(2,1)} %fusion.43), channel_id=1, source_target_pairs={{0,1},{1,2},{2,3},{3,4},{4,5},{5,6},{6,7},{7,0},{8,9},{9,10},{10,1... | collective-permute-start | bytes 786440 | tf_op jit(solution)/shard_map/while/body/eval_jaxpr/ppermute | solution.py:12
  133.1 9.6 %collective-permute-start.1 = (bf16[8,256]{1,0:T(8,128)(2,1)S(1)}, bf16[8,256]{1,0:T(8,128)(2,1)S(1)}, u32[]{:S(2)}, u32[]{:S(2)}) collective-permute-start(bf16[8,256]{1,0:T(8,128)(2,1)S(1)} %get-tuple-element.194), channel_id=1, source_target_pairs={{0,1},{1,2},{2,3},{3,4},{4,5},{5,6},{6,7},{7,0},{8,9},{9,10},{10,1... | collective-permute-start | bytes 12296 | tf_op jit(solution)/shard_map/while/body/eval_jaxpr/ppermute | solution.py:12
  133.2 9.5 %collective-permute-start.2 = (bf16[8,256]{1,0:T(8,128)(2,1)S(1)}, bf16[8,256]{1,0:T(8,128)(2,1)S(1)}, u32[]{:S(2)}, u32[]{:S(2)}) collective-permute-start(bf16[8,256]{1,0:T(8,128)(2,1)S(1)} %get-tuple-element.195), channel_id=1, source_target_pairs={{0,1},{1,2},{2,3},{3,4},{4,5},{5,6},{6,7},{7,0},{8,9},{9,10},{10,1... | collective-permute-start | bytes 12296 | tf_op jit(solution)/shard_map/while/body/eval_jaxpr/ppermute | solution.py:12
  143.8 15.9 %collective-permute-start = (bf16[256,8,64]{0,2,1:T(8,128)(2,1)S(1)}, bf16[256,8,64]{0,2,1:T(8,128)(2,1)S(1)}, u32[]{:S(2)}, u32[]{:S(2)}) collective-permute-start(bf16[256,8,64]{0,2,1:T(8,128)(2,1)S(1)} %copy.58), channel_id=1, source_target_pairs={{0,1},{1,2},{2,3},{3,4},{4,5},{5,6},{6,7},{7,0},{8,9},{9,10},{10,1... | collective-permute-start | bytes 786440 | tf_op jit(solution)/shard_map/while/body/eval_jaxpr/ppermute | solution.py:12
  148.7 10.0 %collective-permute-start.3 = (bf16[256,8,64]{0,2,1:T(8,128)(2,1)}, bf16[256,8,64]{0,2,1:T(8,128)(2,1)}, u32[]{:S(2)}, u32[]{:S(2)}) collective-permute-start(bf16[256,8,64]{0,2,1:T(8,128)(2,1)} %fusion.43), channel_id=1, source_target_pairs={{0,1},{1,2},{2,3},{3,4},{4,5},{5,6},{6,7},{7,0},{8,9},{9,10},{10,1... | collective-permute-start | bytes 786440 | tf_op jit(solution)/shard_map/while/body/eval_jaxpr/ppermute | solution.py:12
  149.1 9.6 %collective-permute-start.1 = (bf16[8,256]{1,0:T(8,128)(2,1)S(1)}, bf16[8,256]{1,0:T(8,128)(2,1)S(1)}, u32[]{:S(2)}, u32[]{:S(2)}) collective-permute-start(bf16[8,256]{1,0:T(8,128)(2,1)S(1)} %get-tuple-element.194), channel_id=1, source_target_pairs={{0,1},{1,2},{2,3},{3,4},{4,5},{5,6},{6,7},{7,0},{8,9},{9,10},{10,1... | collective-permute-start | bytes 12296 | tf_op jit(solution)/shard_map/while/body/eval_jaxpr/ppermute | solution.py:12
  149.2 9.5 %collective-permute-start.2 = (bf16[8,256]{1,0:T(8,128)(2,1)S(1)}, bf16[8,256]{1,0:T(8,128)(2,1)S(1)}, u32[]{:S(2)}, u32[]{:S(2)}) collective-permute-start(bf16[8,256]{1,0:T(8,128)(2,1)S(1)} %get-tuple-element.195), channel_id=1, source_target_pairs={{0,1},{1,2},{2,3},{3,4},{4,5},{5,6},{6,7},{7,0},{8,9},{9,10},{10,1... | collective-permute-start | bytes 12296 | tf_op jit(solution)/shard_map/while/body/eval_jaxpr/ppermute | solution.py:12
  (11 other events, 198.2 us)
where the time goes:
time: 166 us; the launch traced here: 165 us
  waiting for transfers between devices  57.9 us (35%)
  matrix products  44.1 us (27%)
  starting transfers between devices  30.6 us (18%)
  other arithmetic  16.3 us (10%)
  local copies, waits for them, and re-layouts  11.3 us (7%)
  blocking collectives  3.94 us (2%)
    ppermute x32, waiting for transfers between devices, from_behind(): lax.ppermute(array, axis, [(i, (i + by) % peers) for i in range(peers)])  56 us
    ppermute x32, starting transfers between devices, from_behind(): lax.ppermute(array, axis, [(i, (i + by) % peers) for i in range(peers)])  27.1 us
    dot_general x8, matrix products, absorb_block(): jnp.einsum('hqk,khd->qhd', exponent.astype(jnp.bfloat16), value_block, pr...  24.3 us
    dot_general x8, matrix products, absorb_block(): jnp.einsum('qhd,khd->hqk', query, key_block, preferred_element_type=jnp.f...  14.7 us
    convert_element_type x8, other arithmetic, visit(): from_behind(weighted.astype(jnp.bfloat16), 'blk', 1).astype(weighted.dtype)  7.89 us
    dot_general x1, matrix products, project(): projected = jnp.dot(normed, weight, preferred_element_type=jnp.float32)  3.97 us
    all_to_all x1, blocking collectives, per_device(): lax.all_to_all(attended, 'head', split_axis=0, concat_axis=1, tiled=True)  3.94 us
    all_to_all x1, starting transfers between devices, per_device(): lax.all_to_all(stacked, 'head', split_axis=2, concat_axis=0, tiled=True)  3.53 us
  transfers between devices with their start and end apart: 33, of which 9 were waited for; matrix products, arithmetic and copies ran while one was open for 30% of the time, Pallas kernels for 0%

commit v1 on v0

v1 whole, which is shorter than its diff:
```python
import functools

import jax
import jax.numpy as jnp
from jax import lax
from jax.experimental import pallas as pl
from jax.experimental.pallas import tpu as pltpu
from jax.sharding import PartitionSpec as P

H = 16
HD = 64
F32 = jnp.float32
BF16 = jnp.bfloat16


def dot(a, b):
    return jnp.dot(a, b, preferred_element_type=F32)


def dot_nt(a, b):
    return lax.dot_general(a, b, (((1,), (1,)), ((), ())), preferred_element_type=F32)


def kernel(
    n, rows, width,
    patches, ln_gain, gains, w_qkv, w_out, out,
    xg, wq, wk, wv, wvt, wo, qbd, ones, m_ref, l_ref, acc, att, att_in,
    w_sem, ring_send, ring_recv, sib_send, sib_recv, att_send, att_recv,
):
    d = patches.shape[1]
    nq = 2 * rows
    half = rows // 2
    pairs = width // (2 * HD)
    g, c, b = lax.axis_index("group"), lax.axis_index("head"), lax.axis_index("blk")
    odd = b % 2
    up = jnp.where(b == n - 2, n - 1, b + 2)
    down = jnp.where(b == 1, 0, b - 2)
    nxt = jnp.where(odd == 1, down, up)
    up_p = jnp.where(b == n - 1, n - 2, b + 2)
    down_p = jnp.where(b == 0, 1, b - 2)
    prv = jnp.where(odd == 1, up_p, down_p)
    towards = ((g, c, nxt), (g, c, prv))
    sibling = (g, 1 - c, b)

    barrier = pltpu.get_barrier_semaphore()
    for peer in (*towards, sibling):
        pl.semaphore_signal(barrier, inc=1, device_id=peer, device_id_type=pl.DeviceIdType.MESH)

    def fetch(part, target):
        columns = pl.ds(pl.multiple_of(part * d + c * width, 128), width)
        return pltpu.make_async_copy(w_qkv.at[:, columns], target, w_sem.at[part])

    loads = [fetch(0, wq), fetch(1, wk), fetch(2, wv)]
    for load in loads:
        load.start()
    load_out = pltpu.make_async_copy(w_out, wo, w_sem.at[3])
    load_out.start()

    mine = pl.ds(pl.multiple_of(c * rows, rows), rows)
    theirs = pl.ds(pl.multiple_of((1 - c) * rows, rows), rows)

    def piece(k, which):
        return xg.at[k, pl.ds(pl.multiple_of(c * rows + which * half, half), half), :]

    def hop(way, k, source):
        return pltpu.make_async_remote_copy(
            src_ref=source,
            dst_ref=piece(k, way),
            send_sem=ring_send.at[way, k],
            recv_sem=ring_recv.at[way, k],
            device_id=towards[way],
            device_id_type=pl.DeviceIdType.MESH,
        )

    def across(k):
        return pltpu.make_async_remote_copy(
            src_ref=xg.at[k, mine, :],
            dst_ref=xg.at[k, mine, :],
            send_sem=sib_send.at[k],
            recv_sem=sib_recv.at[k],
            device_id=sibling,
            device_id_type=pl.DeviceIdType.MESH,
        )

    def across_in(k):
        return pltpu.make_async_remote_copy(
            src_ref=xg.at[k, theirs, :],
            dst_ref=xg.at[k, theirs, :],
            send_sem=sib_send.at[k],
            recv_sem=sib_recv.at[k],
            device_id=sibling,
            device_id_type=pl.DeviceIdType.MESH,
        )

    x = patches[...].astype(F32)
    centre = x - jnp.mean(x, axis=-1, keepdims=True)
    variance = jnp.mean(centre * centre, axis=-1, keepdims=True)
    xg[0, mine, :] = (centre * lax.rsqrt(variance + 1e-05) * ln_gain[...]).astype(BF16)

    pl.semaphore_wait(barrier, 3)
    across(0).start()
    for h in range(2):
        for way in range(2):
            hop(way, 1 + h, piece(0, h)).start()

    row_id = lax.broadcasted_iota(jnp.int32, (4 * HD, 4 * HD), 0) >> 6
    col_id = lax.broadcasted_iota(jnp.int32, (4 * HD, 4 * HD), 1) >> 6
    ones[...] = jnp.where(row_id == col_id, 1.0, 0.0).astype(BF16)
    m_ref[...] = jnp.full(m_ref.shape, -1e30, F32)
    l_ref[...] = jnp.zeros(l_ref.shape, F32)
    acc[...] = jnp.zeros(acc.shape, F32)
    qbd[...] = jnp.zeros(qbd.shape, BF16)

    def head_norm(columns, gain):
        parts = []
        for i in range(width // (4 * HD)):
            block = columns[:, i * 4 * HD : (i + 1) * 4 * HD]
            total = dot((block * block).astype(BF16), ones[...])
            parts.append(block * lax.rsqrt(total * (1.0 / HD) + 1e-06))
        return jnp.concatenate(parts, axis=1) * gain

    gain_columns = pl.ds(pl.multiple_of(c * width, 128), width)
    gain_q = gains[0:1, gain_columns]
    gain_k = gains[1:2, gain_columns]

    loads[2].wait()
    wvt[...] = wv[...].T
    loads[0].wait()
    across_in(0).wait_recv()
    query = head_norm(dot(xg[0], wq[...]), gain_q).astype(BF16).astype(F32) * (HD ** -0.5)
    for j in range(pairs):
        block = query[:, j * 2 * HD : (j + 1) * 2 * HD].T.astype(BF16)
        qbd[j, 0:HD, 0:nq] = block[0:HD]
        qbd[j, HD : 2 * HD, nq : 2 * nq] = block[HD : 2 * HD]
    loads[1].wait()

    def absorb(k):
        tokens = xg[k]
        keys = head_norm(dot(tokens, wk[...]), gain_k).astype(BF16)
        values_t = dot_nt(wvt[...], tokens).astype(BF16)
        for j in range(pairs):
            scores = dot(keys[:, j * 2 * HD : (j + 1) * 2 * HD], qbd[j])
            old = m_ref[j]
            new = jnp.maximum(old, jnp.max(scores, axis=0, keepdims=True))
            shrink = jnp.exp(old - new)
            weights = jnp.exp(scores - new)
            m_ref[j] = new
            l_ref[j] = l_ref[j] * shrink + jnp.sum(weights, axis=0, keepdims=True)
            weights = weights.astype(BF16)
            for e in range(2):
                channels = slice((2 * j + e) * HD, (2 * j + e + 1) * HD)
                span = slice(e * nq, (e + 1) * nq)
                acc[channels, :] = acc[channels, :] * shrink[:, span] + dot(
                    values_t[channels], weights[:, span]
                )

    absorb(0)

    def step(k, carry):
        for way in range(2):
            hop(way, k, piece(k, way)).wait_recv()

            @pl.when(k < n - 3)
            def _():
                hop(way, k + 2, piece(k, way)).start()

            @pl.when(k == n - 3 + way)
            def _():
                hop(way, n - 1, piece(k, way)).start()

        across(k).start()

        @pl.when(k >= 2)
        def _():
            across_in(k - 1).wait_recv()
            absorb(k - 1)

        return carry

    lax.fori_loop(1, n, step, 0)
    across_in(n - 1).wait_recv()
    absorb(n - 1)

    for j in range(pairs):
        inverse = 1.0 / l_ref[j]
        for e in range(2):
            channels = slice((2 * j + e) * HD, (2 * j + e + 1) * HD)
            acc[channels, :] = acc[channels, :] * inverse[:, e * nq : (e + 1) * nq]
        both = slice(2 * j * HD, 2 * (j + 1) * HD)
        att[:, both] = acc[both, :].T.astype(BF16)
    swap = pltpu.make_async_remote_copy(
        src_ref=att.at[theirs, :],
        dst_ref=att_in,
        send_sem=att_send,
        recv_sem=att_recv,
        device_id=sibling,
        device_id_type=pl.DeviceIdType.MESH,
    )
    swap.start()
    load_out.wait()
    my_heads = pl.ds(pl.multiple_of(c * width, width), width)
    their_heads = pl.ds(pl.multiple_of((1 - c) * width, width), width)
    partial = dot(att[mine, :], wo[my_heads, :])
    swap.wait_recv()
    out[...] = (partial + dot(att_in[...], wo[their_heads, :])).astype(BF16)

    swap.wait_send()
    across(0).wait_send()

    def drain(k, carry):
        for way in range(2):
            hop(way, k, piece(k, way)).wait_send()
        across(k).wait_send()
        return carry

    lax.fori_loop(1, n, drain, 0)


def per_device(patches, ln_gain, w_qkv, qk_gains, w_out):
    rows, d = patches.shape
    n = lax.axis_size("blk")
    width = H // lax.axis_size("head") * HD
    nq = 2 * rows
    vmem = pl.BlockSpec(memory_space=pltpu.VMEM)
    hbm = pl.BlockSpec(memory_space=pl.ANY)
    return pl.pallas_call(
        functools.partial(kernel, n, rows, width),
        out_shape=jax.ShapeDtypeStruct((rows, d), BF16),
        in_specs=[vmem, vmem, vmem, hbm, hbm],
        out_specs=vmem,
        scratch_shapes=[
            pltpu.VMEM((n, nq, d), BF16),
            pltpu.VMEM((d, width), BF16),
            pltpu.VMEM((d, width), BF16),
            pltpu.VMEM((d, width), BF16),
            pltpu.VMEM((width, d), BF16),
            pltpu.VMEM((d, d), BF16),
            pltpu.VMEM((width // (2 * HD), 2 * HD, 2 * nq), BF16),
            pltpu.VMEM((4 * HD, 4 * HD), BF16),
            pltpu.VMEM((width // (2 * HD), 1, 2 * nq), F32),
            pltpu.VMEM((width // (2 * HD), 1, 2 * nq), F32),
            pltpu.VMEM((width, nq), F32),
            pltpu.VMEM((nq, width), BF16),
            pltpu.VMEM((rows, width), BF16),
            pltpu.SemaphoreType.DMA((4,)),
            pltpu.SemaphoreType.DMA((2, n)),
            pltpu.SemaphoreType.DMA((2, n)),
            pltpu.SemaphoreType.DMA((n,)),
            pltpu.SemaphoreType.DMA((n,)),
            pltpu.SemaphoreType.DMA,
            pltpu.SemaphoreType.DMA,
        ],
        compiler_params=pltpu.CompilerParams(
            collective_id=0, has_side_effects=True, vmem_limit_bytes=48 << 20
        ),
    )(patches, ln_gain.reshape(1, d), qk_gains, w_qkv, w_out)


def solution(mesh):
    placed = (P(("group", "head", "blk"), None), P(), P(), P(), P())
    return jax.shard_map(
        per_device,
        mesh=mesh,
        in_specs=placed,
        out_specs=P(("group", "head", "blk"), None),
        check_vma=False,
    )
```

time: 166 us -> 38.2 us (0.23)
  waiting for transfers between devices: 57.9 us -> 0 us
  matrix products: 44.1 us -> 0 us
  Pallas kernels: 0 us -> 33 us
  starting transfers between devices: 30.6 us -> 0 us
  other arithmetic: 16.3 us -> 0 us
  local copies, waits for them, and re-layouts: 11.3 us -> 4.63 us
  blocking collectives: 3.94 us -> 0 us
    ppermute x32 -> x0, waiting for transfers between devices: 56 us -> none  [from_behind(): lax.ppermute(array, axis, [(i, (i + by) % peers) for i in range(peers)])]
    dot_general x18 -> x0, matrix products: 44.1 us -> none  [the longest x8 24.3 us: absorb_block(): jnp.einsum('hqk,khd->qhd', exponent.astype(jnp.bfloat16), value_block, pr...]
    pallas_call x0 -> x1, Pallas kernels: none -> 33 us  [per_device(): pl.pallas_call(functools.partial(kernel, n, rows, width), out_shape=jax.S...]
    ppermute x32 -> x0, starting transfers between devices: 27.1 us -> none  [from_behind(): lax.ppermute(array, axis, [(i, (i + by) % peers) for i in range(peers)])]
    convert_element_type x34 -> x0, other arithmetic: 8.45 us -> none  [the longest x8 7.89 us: visit(): from_behind(weighted.astype(jnp.bfloat16), 'blk', 1).astype(weighted.dtype)]
    reduce_sum x12 -> x0, other arithmetic: 6.36 us -> none  [the longest x8 2.85 us: absorb_block(): running_sum = running_sum * shrink + jnp.sum(exponent, axis=-1)]
    all_to_all x1 -> x0, blocking collectives: 3.94 us -> none  [per_device(): lax.all_to_all(attended, 'head', split_axis=0, concat_axis=1, tiled=True)]
    all_to_all x1 -> x0, starting transfers between devices: 3.53 us -> none  [per_device(): lax.all_to_all(stacked, 'head', split_axis=2, concat_axis=0, tiled=True)]
  transfers between devices with their start and end apart: 33 -> 0, of which waited for: 9 -> 0; matrix products, arithmetic and copies ran while one was open for 30% -> 0% of each run, Pallas kernels for 0% -> 0%
where the time goes in v1:
time: 38.2 us; the launch traced here: 37.6 us
  Pallas kernels  33 us (86%)
  local copies, waits for them, and re-layouts  4.63 us (12%)
    pallas_call x1, Pallas kernels, per_device(): pl.pallas_call(functools.partial(kernel, n, rows, width), out_shape=jax.S...  33 us
    unnamed x9, local copies, waits for them, and re-layouts  4.63 us

profile of v1, /device:TPU:0, one launch (start us, length us, event | category | flops | bytes accessed | tf_op | source)
XLA Modules:
  0.0 37.6 jit_solution(4346874804429325090)
XLA Ops:
  0.0 0.0 copy-start
  0.0 1.6 %copy-done = bf16[1024,1024]{1,0:T(8,128)(2,1)S(1)} copy-done((bf16[1024,1024]{1,0:T(8,128)(2,1)S(1)}, bf16[1024,1024]{1,0:T(8,128)(2,1)}, u32[]{:S(2)}) %copy-start) | copy-done | bytes 2097176
  1.6 0.0 copy-start.1
  1.6 0.9 %copy-done.1 = bf16[128,1024]{1,0:T(8,128)(2,1)S(1)} copy-done((bf16[128,1024]{1,0:T(8,128)(2,1)S(1)}, bf16[128,1024]{1,0:T(8,128)(2,1)}, u32[]{:S(2)}) %copy-start.1) | copy-done | bytes 262168
  2.5 0.0 copy-start.2
  2.5 0.7 %copy-done.2 = f32[2,1024]{1,0:T(2,128)S(1)} copy-done((f32[2,1024]{1,0:T(2,128)S(1)}, f32[2,1024]{1,0:T(2,128)}, u32[]{:S(2)}) %copy-start.2) | copy-done | bytes 8216
  3.2 0.0 copy-start.3
  3.2 0.7 %copy-done.3 = f32[1024]{0:T(1024)S(1)} copy-done((f32[1024]{0:T(1024)S(1)}, f32[1024]{0:T(1024)}, u32[]{:S(2)}) %copy-start.3) | copy-done | bytes 4120
  3.9 33.0 %shard_map.55 = bf16[128,1024]{1,0:T(8,128)(2,1)S(1)} custom-call(bf16[128,1024]{1,0:T(8,128)(2,1)S(1)} %copy-done.1, f32[1,1024]{1,0:T(1,128)S(1)} %bitcast.1, f32[2,1024]{1,0:T(2,128)S(1)} %copy-done.2, bf16[1024,3072]{1,0:T(8,128)(2,1)} %w_qkv.1, bf16[1024,1024]{1,0:T(8,128)(2,1)S(1)} %copy-done), custom_call_target="tpu_custom_call" | custom-call | tf_op jit(solution)/shard_map/pallas_call | solution.py:226
  36.9 0.7 %copy.7 = bf16[128,1024]{1,0:T(8,128)(2,1)} copy(bf16[128,1024]{1,0:T(8,128)(2,1)S(1)} %shard_map.55) | data formatting | bytes 524288
Async XLA Ops:
  0.0 1.6 %copy-start = (bf16[1024,1024]{1,0:T(8,128)(2,1)S(1)}, bf16[1024,1024]{1,0:T(8,128)(2,1)}, u32[]{:S(2)}) copy-start(bf16[1024,1024]{1,0:T(8,128)(2,1)} %w_out.1) | copy-start | bytes 6291460
  1.6 0.9 %copy-start.1 = (bf16[128,1024]{1,0:T(8,128)(2,1)S(1)}, bf16[128,1024]{1,0:T(8,128)(2,1)}, u32[]{:S(2)}) copy-start(bf16[128,1024]{1,0:T(8,128)(2,1)} %patches.1) | copy-start | bytes 786436
  2.5 0.7 %copy-start.2 = (f32[2,1024]{1,0:T(2,128)S(1)}, f32[2,1024]{1,0:T(2,128)}, u32[]{:S(2)}) copy-start(f32[2,1024]{1,0:T(2,128)} %gains.1) | copy-start | bytes 24580
  3.2 0.7 %copy-start.3 = (f32[1024]{0:T(1024)S(1)}, f32[1024]{0:T(1024)}, u32[]{:S(2)}) copy-start(f32[1024]{0:T(1024)} %param.6) | copy-start | bytes 12292

commit v2 on v1

--- a/solution.py
+++ b/solution.py
@@ -23,11 +23,11 @@
 
 def kernel(
     n, rows, width,
-    patches, ln_gain, gains, w_qkv, w_out, out,
-    xg, wq, wk, wv, wvt, wo, qbd, ones, m_ref, l_ref, acc, att, att_in,
+    patches_hbm, ln_gain_hbm, gains_hbm, w_qkv, w_out, out,
+    patches, ln_gain, gains, xg, wq, wk, wv, wvt, wo, qbd, ones, m_ref, l_ref, acc, att, att_in,
     w_sem, ring_send, ring_recv, sib_send, sib_recv, att_send, att_recv,
 ):
-    d = patches.shape[1]
+    d = patches_hbm.shape[1]
     nq = 2 * rows
     half = rows // 2
     pairs = width // (2 * HD)
@@ -42,6 +42,14 @@
     towards = ((g, c, nxt), (g, c, prv))
     sibling = (g, 1 - c, b)
 
+    small = [
+        pltpu.make_async_copy(source, target, w_sem.at[4 + i])
+        for i, (source, target) in enumerate(
+            ((patches_hbm, patches), (ln_gain_hbm, ln_gain), (gains_hbm, gains))
+        )
+    ]
+    for load in small:
+        load.start()
     barrier = pltpu.get_barrier_semaphore()
     for peer in (*towards, sibling):
         pl.semaphore_signal(barrier, inc=1, device_id=peer, device_id_type=pl.DeviceIdType.MESH)
@@ -92,6 +100,8 @@
             device_id_type=pl.DeviceIdType.MESH,
         )
 
+    small[0].wait()
+    small[1].wait()
     x = patches[...].astype(F32)
     centre = x - jnp.mean(x, axis=-1, keepdims=True)
     variance = jnp.mean(centre * centre, axis=-1, keepdims=True)
@@ -120,6 +130,7 @@
         return jnp.concatenate(parts, axis=1) * gain
 
     gain_columns = pl.ds(pl.multiple_of(c * width, 128), width)
+    small[2].wait()
     gain_q = gains[0:1, gain_columns]
     gain_k = gains[1:2, gain_columns]
 
@@ -154,9 +165,7 @@
                     values_t[channels], weights[:, span]
                 )
 
-    absorb(0)
-
-    def step(k, carry):
+    def receive(k):
         for way in range(2):
             hop(way, k, piece(k, way)).wait_recv()
 
@@ -170,16 +179,24 @@
 
         across(k).start()
 
+    def step(k, carry):
+        @pl.when(k < n - 1)
+        def _():
+            receive(k)
+
         @pl.when(k >= 2)
         def _():
             across_in(k - 1).wait_recv()
-            absorb(k - 1)
+
+        absorb(k - 1)
+
+        @pl.when(k == n - 1)
+        def _():
+            receive(k)
 
         return carry
 
-    lax.fori_loop(1, n, step, 0)
-    across_in(n - 1).wait_recv()
-    absorb(n - 1)
+    lax.fori_loop(1, n + 1, step, 0)
 
     for j in range(pairs):
         inverse = 1.0 / l_ref[j]
@@ -222,13 +239,16 @@
     width = H // lax.axis_size("head") * HD
     nq = 2 * rows
     vmem = pl.BlockSpec(memory_space=pltpu.VMEM)
-    hbm = pl.BlockSpec(memory_space=pl.ANY)
+    hbm = pl.BlockSpec(memory_space=pltpu.HBM)
     return pl.pallas_call(
         functools.partial(kernel, n, rows, width),
         out_shape=jax.ShapeDtypeStruct((rows, d), BF16),
-        in_specs=[vmem, vmem, vmem, hbm, hbm],
+        in_specs=[hbm, hbm, hbm, hbm, hbm],
         out_specs=vmem,
         scratch_shapes=[
+            pltpu.VMEM((rows, d), BF16),
+            pltpu.VMEM((1, d), F32),
+            pltpu.VMEM((2, d), F32),
             pltpu.VMEM((n, nq, d), BF16),
             pltpu.VMEM((d, width), BF16),
             pltpu.VMEM((d, width), BF16),
@@ -242,7 +262,7 @@
             pltpu.VMEM((width, nq), F32),
             pltpu.VMEM((nq, width), BF16),
             pltpu.VMEM((rows, width), BF16),
-            pltpu.SemaphoreType.DMA((4,)),
+            pltpu.SemaphoreType.DMA((7,)),
             pltpu.SemaphoreType.DMA((2, n)),
             pltpu.SemaphoreType.DMA((2, n)),
             pltpu.SemaphoreType.DMA((n,)),
@@ -251,7 +271,7 @@
             pltpu.SemaphoreType.DMA,
         ],
         compiler_params=pltpu.CompilerParams(
-            collective_id=0, has_side_effects=True, vmem_limit_bytes=48 << 20
+            collective_id=0, has_side_effects=True, vmem_limit_bytes=56 << 20
         ),
     )(patches, ln_gain.reshape(1, d), qk_gains, w_qkv, w_out)
 

time: 38.2 us -> 36.2 us (0.948); the launches traced: 37.6 us -> 36.1 us
  local copies, waits for them, and re-layouts: 4.63 us -> 1.67 us
  Pallas kernels: 33 us -> 34.4 us
    unnamed x9 -> x1, local copies, waits for them, and re-layouts: 4.63 us -> 1.67 us
    pallas_call x1, Pallas kernels: 33 us -> 34.4 us  [per_device(): pl.pallas_call(functools.partial(kernel, n, rows, width), out_shape=jax.S...]
where the time goes in v2:
time: 36.2 us; the launch traced here: 36.1 us
  Pallas kernels  34.4 us (95%)
  local copies, waits for them, and re-layouts  1.67 us (5%)
    pallas_call x1, Pallas kernels, per_device(): pl.pallas_call(functools.partial(kernel, n, rows, width), out_shape=jax.S...  34.4 us
    unnamed x1, local copies, waits for them, and re-layouts  1.67 us

profile of v2, /device:TPU:0, one launch (start us, length us, event | category | flops | bytes accessed | tf_op | source)
XLA Modules:
  0.0 36.1 jit_solution(11837211737181135792)
XLA Ops:
  0.0 34.4 %shard_map.55 = bf16[128,1024]{1,0:T(8,128)(2,1)} custom-call(bf16[128,1024]{1,0:T(8,128)(2,1)} %patches_hbm.1, f32[1,1024]{1,0:T(1,128)} %bitcast.1, f32[2,1024]{1,0:T(2,128)} %gains_hbm.1, bf16[1024,3072]{1,0:T(8,128)(2,1)} %w_qkv.1, bf16[1024,1024]{1,0:T(8,128)(2,1)} %w_out.1), custom_call_target="tpu_custom_call" | custom-call | tf_op jit(solution)/shard_map/pallas_call | solution.py:243
  34.4 1.7 %copy.7 = bf16[128,1024]{1,0:T(8,128)(2,1)} copy(bf16[128,1024]{1,0:T(8,128)(2,1)} %shard_map.55) | data formatting | bytes 524288

commit v3 on v2

--- a/solution.py
+++ b/solution.py
@@ -9,6 +9,7 @@
 
 H = 16
 HD = 64
+PARTS = 2
 F32 = jnp.float32
 BF16 = jnp.bfloat16
 
@@ -30,6 +31,7 @@
     d = patches_hbm.shape[1]
     nq = 2 * rows
     half = rows // 2
+    sub = half // PARTS
     pairs = width // (2 * HD)
     g, c, b = lax.axis_index("group"), lax.axis_index("head"), lax.axis_index("blk")
     odd = b % 2
@@ -67,15 +69,16 @@
     mine = pl.ds(pl.multiple_of(c * rows, rows), rows)
     theirs = pl.ds(pl.multiple_of((1 - c) * rows, rows), rows)
 
-    def piece(k, which):
-        return xg.at[k, pl.ds(pl.multiple_of(c * rows + which * half, half), half), :]
-
-    def hop(way, k, source):
+    def piece(k, which, part):
+        first = pl.multiple_of(c * rows + which * half + part * sub, sub)
+        return xg.at[k, pl.ds(first, sub), :]
+
+    def hop(way, k, part, source):
         return pltpu.make_async_remote_copy(
             src_ref=source,
-            dst_ref=piece(k, way),
-            send_sem=ring_send.at[way, k],
-            recv_sem=ring_recv.at[way, k],
+            dst_ref=piece(k, way, part),
+            send_sem=ring_send.at[way, k, part],
+            recv_sem=ring_recv.at[way, k, part],
             device_id=towards[way],
             device_id_type=pl.DeviceIdType.MESH,
         )
@@ -110,8 +113,9 @@
     pl.semaphore_wait(barrier, 3)
     across(0).start()
     for h in range(2):
-        for way in range(2):
-            hop(way, 1 + h, piece(0, h)).start()
+        for part in range(PARTS):
+            for way in range(2):
+                hop(way, 1 + h, part, piece(0, h, part)).start()
 
     row_id = lax.broadcasted_iota(jnp.int32, (4 * HD, 4 * HD), 0) >> 6
     col_id = lax.broadcasted_iota(jnp.int32, (4 * HD, 4 * HD), 1) >> 6
@@ -145,8 +149,7 @@
         qbd[j, HD : 2 * HD, nq : 2 * nq] = block[HD : 2 * HD]
     loads[1].wait()
 
-    def absorb(k):
-        tokens = xg[k]
+    def absorb_rows(tokens):
         keys = head_norm(dot(tokens, wk[...]), gain_k).astype(BF16)
         values_t = dot_nt(wvt[...], tokens).astype(BF16)
         for j in range(pairs):
@@ -165,22 +168,26 @@
                     values_t[channels], weights[:, span]
                 )
 
+    def absorb(k):
+        absorb_rows(xg[k])
+
     def receive(k):
-        for way in range(2):
-            hop(way, k, piece(k, way)).wait_recv()
-
-            @pl.when(k < n - 3)
-            def _():
-                hop(way, k + 2, piece(k, way)).start()
-
-            @pl.when(k == n - 3 + way)
-            def _():
-                hop(way, n - 1, piece(k, way)).start()
+        for part in range(PARTS):
+            for way in range(2):
+                hop(way, k, part, piece(k, way, part)).wait_recv()
+
+                @pl.when(k < n - 3)
+                def _():
+                    hop(way, k + 2, part, piece(k, way, part)).start()
+
+                @pl.when(k == n - 3 + way)
+                def _():
+                    hop(way, n - 1, part, piece(k, way, part)).start()
 
         across(k).start()
 
     def step(k, carry):
-        @pl.when(k < n - 1)
+        @pl.when((k >= 2) & (k < n - 1))
         def _():
             receive(k)
 
@@ -190,13 +197,24 @@
 
         absorb(k - 1)
 
-        @pl.when(k == n - 1)
+        @pl.when((k == 1) | (k == n - 1))
         def _():
             receive(k)
 
         return carry
 
-    lax.fori_loop(1, n + 1, step, 0)
+    lax.fori_loop(1, n, step, 0)
+
+    def last(i, carry):
+        @pl.when(i == 1)
+        def _():
+            across_in(n - 1).wait_recv()
+
+        first = (c + i - 2 * c * i) * rows
+        absorb_rows(xg[n - 1, pl.ds(pl.multiple_of(first, rows), rows), :])
+        return carry
+
+    lax.fori_loop(0, 2, last, 0)
 
     for j in range(pairs):
         inverse = 1.0 / l_ref[j]
@@ -225,8 +243,9 @@
     across(0).wait_send()
 
     def drain(k, carry):
-        for way in range(2):
-            hop(way, k, piece(k, way)).wait_send()
+        for part in range(PARTS):
+            for way in range(2):
+                hop(way, k, part, piece(k, way, part)).wait_send()
         across(k).wait_send()
         return carry
 
@@ -263,8 +282,8 @@
             pltpu.VMEM((nq, width), BF16),
             pltpu.VMEM((rows, width), BF16),
             pltpu.SemaphoreType.DMA((7,)),
-            pltpu.SemaphoreType.DMA((2, n)),
-            pltpu.SemaphoreType.DMA((2, n)),
+            pltpu.SemaphoreType.DMA((2, n, PARTS)),
+            pltpu.SemaphoreType.DMA((2, n, PARTS)),
             pltpu.SemaphoreType.DMA((n,)),
             pltpu.SemaphoreType.DMA((n,)),
             pltpu.SemaphoreType.DMA,

time: 36.2 us -> 35.5 us (0.981)
  Pallas kernels: 34.4 us -> 33.4 us
    pallas_call x1, Pallas kernels: 34.4 us -> 33.4 us  [per_device(): pl.pallas_call(functools.partial(kernel, n, rows, width), out_shape=jax.S...]
where the time goes in v3:
time: 35.5 us; the launch traced here: 35 us
  Pallas kernels  33.4 us (94%)
  local copies, waits for them, and re-layouts  1.67 us (5%)
    pallas_call x1, Pallas kernels, per_device(): pl.pallas_call(functools.partial(kernel, n, rows, width), out_shape=jax.S...  33.4 us
    unnamed x1, local copies, waits for them, and re-layouts  1.67 us

profile of v3, /device:TPU:0, one launch (start us, length us, event | category | flops | bytes accessed | tf_op | source)
XLA Modules:
  0.0 35.0 jit_solution(3622287439871523696)
XLA Ops:
  0.0 33.4 %shard_map.55 = bf16[128,1024]{1,0:T(8,128)(2,1)} custom-call(bf16[128,1024]{1,0:T(8,128)(2,1)} %patches_hbm.1, f32[1,1024]{1,0:T(1,128)} %bitcast.1, f32[2,1024]{1,0:T(2,128)} %gains_hbm.1, bf16[1024,3072]{1,0:T(8,128)(2,1)} %w_qkv.1, bf16[1024,1024]{1,0:T(8,128)(2,1)} %w_out.1), custom_call_target="tpu_custom_call" | custom-call | tf_op jit(solution)/shard_map/pallas_call | solution.py:262
  33.4 1.7 %copy.7 = bf16[128,1024]{1,0:T(8,128)(2,1)} copy(bf16[128,1024]{1,0:T(8,128)(2,1)} %shard_map.55) | data formatting | bytes 524288
